TPU v7x, 256 devices: a whole 4x4x8 slice. The times are simulated.
256 devices in a mesh: section: 2 (over y_lo), dp: 16 (over z, y_hi), tensor: 8 (over x, core).
Axes of the slice: x: 4, y: 4 (y_hi: 2, y_lo: 2; y = y_hi * 2 + y_lo), z: 8, core: 2. Of those that a mesh axis runs over, the one named last changes fastest.
Arguments:
- fwd_in: bfloat16 [2, 1024, 8192], P('section', 'tensor', 'dp'), may hold values from -6 to 6
- grad_in: bfloat16 [2, 1024, 8192], P('section', 'tensor', 'dp'), may hold values from -6 to 6
- saved_gate: bfloat16 [2, 1024, 14336], P('section', 'dp', 'tensor'), may hold values from -8 to 8
- saved_up: bfloat16 [2, 1024, 14336], P('section', 'dp', 'tensor'), may hold values from -6 to 6
- gate_weight: bfloat16 [2, 8192, 14336], P('section', 'dp', 'tensor'), may hold values from -0.0625 to 0.0625
- up_weight: bfloat16 [2, 8192, 14336], P('section', 'dp', 'tensor'), may hold values from -0.0625 to 0.0625
- down_weight: bfloat16 [2, 14336, 8192], P('section', 'tensor', 'dp'), may hold values from -0.046875 to 0.046875
Outputs:
- fwd_out: bfloat16 [2, 1024, 8192], P('section', 'tensor', 'dp')
- bwd_out: bfloat16 [2, 1024, 8192], P('section', 'tensor', 'dp')
- handed: bfloat16 [2, 1024, 8192], P('section', 'tensor', 'dp')
All inputs are finite; a program needn't handle non-finite values.
Results may differ from a plain program's by a relative error of at most 0.022.
Values may be sent and summed in bfloat16 or wider, within the bound.
No kernel may reach another device: no remote copies, remote signals or barrier semaphores. Data moves between devices by JAX's collectives and lax.ppermute only.
A program may use at most 128 MiB of HBM per device.

v0:
```python
import jax
import jax.numpy as jnp
from jax import lax
from jax.sharding import PartitionSpec as P


def partner(shard, axis, apart):
    return lax.ppermute(shard, axis, [(i, i ^ 1 << apart) for i in range(lax.axis_size(axis))])


def across_rows(part):
    return lax.all_gather(part, "tensor", axis=0, tiled=True)


def feature_total(term):
    return lax.psum_scatter(term, "tensor", scatter_dimension=0, tiled=True)


def transposed(left, right):
    return lax.dot_general(
        left, right, (((1,), (1,)), ((), ())), preferred_element_type=jnp.float32
    )


def local(fwd_in, grad_in, saved_gate, saved_up, gate_weight, up_weight, down_weight):
    inputs = fwd_in[0]
    grads = grad_in[0]
    w_gate = gate_weight[0]
    w_up = up_weight[0]
    w_down = down_weight[0]
    hidden_cols = w_gate.shape[1]
    all_inputs = across_rows(inputs)
    both = jnp.concatenate(
        [
            jnp.dot(all_inputs, w_gate, preferred_element_type=jnp.float32),
            jnp.dot(all_inputs, w_up, preferred_element_type=jnp.float32),
        ],
        axis=1,
    )
    total = lax.psum(both.astype(jnp.bfloat16), "dp").astype(jnp.float32)
    hidden = (jax.nn.silu(total[:, :hidden_cols]) * total[:, hidden_cols:]).astype(jnp.bfloat16)
    mixed_term = jnp.dot(hidden, w_down, preferred_element_type=jnp.float32)
    mixed = feature_total(mixed_term)
    forward_result = (inputs.astype(jnp.float32) + mixed).astype(jnp.bfloat16)
    all_grads = across_rows(grads)
    slope = lax.psum_scatter(
        transposed(all_grads, w_down).astype(jnp.bfloat16), "dp", scatter_dimension=0, tiled=True
    ).astype(jnp.float32)
    gvals = saved_gate[0].astype(jnp.float32)
    uvals = saved_up[0].astype(jnp.float32)
    sig = jax.nn.sigmoid(gvals)
    gate_grad = (slope * uvals * sig * (1.0 + gvals * (1.0 - sig))).astype(jnp.bfloat16)
    up_grad = (slope * gvals * sig).astype(jnp.bfloat16)
    pieces = lax.all_gather((gate_grad, up_grad), "dp", axis=0, tiled=True)
    back_term = transposed(pieces[0], w_gate) + transposed(pieces[1], w_up)
    back = feature_total(back_term)
    backward_result = (grads.astype(jnp.float32) + back).astype(jnp.bfloat16)
    position = lax.axis_index("section")
    outgoing = jnp.where(position == 0, forward_result, backward_result)
    received = partner(outgoing, "section", 0)
    return (forward_result[None], backward_result[None], received[None])


def solution(mesh):
    placed = (
        P("section", "tensor", "dp"),
        P("section", "tensor", "dp"),
        P("section", "dp", "tensor"),
        P("section", "dp", "tensor"),
        P("section", "dp", "tensor"),
        P("section", "dp", "tensor"),
        P("section", "tensor", "dp"),
    )
    return jax.shard_map(
        local,
        mesh=mesh,
        in_specs=placed,
        out_specs=(
            P("section", "tensor", "dp"),
            P("section", "tensor", "dp"),
            P("section", "tensor", "dp"),
        ),
        check_vma=False,
    )
```

profile of v0, /device:TPU:8, one launch (start us, length us, event | category | flops | bytes accessed | tf_op | source)
XLA Modules:
  0.0 895.1 jit_solution(7980363948949293183)
XLA Ops:
  7.2 0.7 all-gather.13.cloned.1.call-update
  8.0 0.7 all-gather.11.cloned.1.call-update
  8.7 0.0 reduce-scatter.6.cloned.1.call-start
  8.7 30.0 %all-gather.13.cloned.1.call-done = bf16[1,1024,512]{2,1,0:T(8,128)(2,1)} async-done(((bf16[1,128,512]{2,1,0:T(8,128)(2,1)}), bf16[1,1024,512]{2,1,0:T(8,128)(2,1)}) %all-gather.13.cloned.1.call-update) | async-done | bytes 1048592 | tf_op jit(solution)/shard_map/all_gather | solution.py:12
  38.7 5.2 convolution_convert_fusion
  43.9 0.0 all-reduce.2.cloned.1.call-start
  44.0 22.4 %all-gather.11.cloned.1.call-done = bf16[1,1024,512]{2,1,0:T(8,128)(2,1)} async-done(((bf16[1,128,512]{2,1,0:T(8,128)(2,1)}), bf16[1,1024,512]{2,1,0:T(8,128)(2,1)}) %all-gather.11.cloned.1.call-update) | async-done | bytes 1048592 | tf_op jit(solution)/shard_map/all_gather | solution.py:12
  66.4 5.9 convolution_convert_fusion.1
  72.3 3.9 convolution_convert_fusion.2
  76.2 6.6 pad_maximum_fusion
  82.8 0.0 all-gather.9.cloned.1.call-start
  82.9 198.7 %reduce-scatter.6.cloned.1.call-done = bf16[64,1792]{1,0:T(8,128)(2,1)} async-done(((bf16[1024,1792]{1,0:T(8,128)(2,1)}), bf16[64,1792]{1,0:T(8,128)(2,1)}) %reduce-scatter.6.cloned.1.call-update) | async-done | bytes 229392 | tf_op jit(solution)/shard_map/reduce_scatter | solution.py:46
  281.6 2.0 fusion.19
  283.7 0.0 all-gather.7.cloned.1.call-start
  283.7 0.5 all-gather.7.cloned.1.call-update
  284.2 0.0 reduce-scatter.4.cloned.1.call-start
  284.3 325.9 %all-reduce.2.cloned.1.call-done = bf16[1024,3584]{1,0:T(8,128)(2,1)} async-done(((bf16[1024,3584]{1,0:T(8,128)(2,1)}), bf16[1024,3584]{1,0:T(8,128)(2,1)}) %all-reduce.2.cloned.1.call-update) | async-done | bytes 7340048 | tf_op jit(solution)/shard_map/psum | solution.py:40
  610.2 10.3 %convert_element_type.44 = f32[1024,3584]{1,0:T(8,128)} convert(bf16[1024,3584]{1,0:T(8,128)(2,1)} %all-reduce.2.cloned.1.call-done) | non-fusion elementwise | flops 3670016 | bytes 22020096 | tf_op jit(solution)/shard_map/convert_element_type | solution.py:40
  620.5 8.6 fusion.1
  629.1 0.0 reduce-scatter.8.cloned.1.call-start
  629.2 82.3 %all-gather.9.cloned.1.call-done = bf16[1024,1792]{1,0:T(8,128)(2,1)} async-done(((bf16[64,1792]{1,0:T(8,128)(2,1)}), bf16[1024,1792]{1,0:T(8,128)(2,1)}) %all-gather.9.cloned.1.call-update) | async-done | bytes 3670032 | tf_op jit(solution)/shard_map/all_gather | solution.py:54
  711.5 6.0 fusion.5
  717.5 89.9 %all-gather.7.cloned.1.call-done = bf16[1024,1792]{1,0:T(8,128)(2,1)} async-done(((bf16[64,1792]{1,0:T(8,128)(2,1)}), bf16[1024,1792]{1,0:T(8,128)(2,1)}) %all-gather.7.cloned.1.call-update) | async-done | bytes 3670032 | tf_op jit(solution)/shard_map/all_gather | solution.py:54
  807.4 6.7 fusion.11
  814.1 29.6 %reduce-scatter.4.cloned.1.call-done = f32[128,512]{1,0:T(8,128)} async-done(((f32[1024,512]{1,0:T(8,128)}), f32[128,512]{1,0:T(8,128)}) %reduce-scatter.4.cloned.1.call-update) | async-done | bytes 262160 | tf_op jit(solution)/shard_map/reduce_scatter | solution.py:16
  843.7 1.6 fusion.29
  845.3 36.1 %reduce-scatter.8.cloned.1.call-done = f32[128,512]{1,0:T(8,128)} async-done(((f32[1024,512]{1,0:T(8,128)}), f32[128,512]{1,0:T(8,128)}) %reduce-scatter.8.cloned.1.call-update) | async-done | bytes 262160 | tf_op jit(solution)/shard_map/reduce_scatter | solution.py:16
  881.5 1.1 broadcast_select_fusion
  882.6 0.7 collective-permute-start
  883.2 1.6 fusion.30
  884.8 2.8 collective-permute-done
  887.6 0.7 copy.12
  (21 shorter events, 0.2 us)
Async XLA Ops:
  7.2 31.5 %copy-start = (bf16[1,1792,512]{2,1,0:T(8,128)(2,1)S(1)}, bf16[1,1792,512]{2,1,0:T(8,128)(2,1)}, u32[]{:S(2)}) copy-start(bf16[1,1792,512]{2,1,0:T(8,128)(2,1)} %param.13) | copy-start | bytes 5505028
  7.2 31.5 %all-gather.13.cloned.1.call-start = ((), (), s32[]{:S(2)}) async-start(), calls=%async_computation.10 | async-start | bytes 1179648 | tf_op jit(solution)/shard_map/all_gather | solution.py:12
  7.9 58.4 %all-gather.11.cloned.1.call-start = ((), (), s32[]{:S(2)}) async-start(), calls=%async_computation.9 | async-start | bytes 1179648 | tf_op jit(solution)/shard_map/all_gather | solution.py:12
  8.7 273.0 %reduce-scatter.6.cloned.1.call-start = ((), (), s32[]{:S(2)}) async-start(), calls=%async_computation.5 | async-start | bytes 3899392 | tf_op jit(solution)/shard_map/reduce_scatter | solution.py:46
  43.9 566.3 %all-reduce.2.cloned.1.call-start = ((), (), s32[]{:S(2)}) async-start(), calls=%async_computation.3 | async-start | bytes 14680064 | tf_op jit(solution)/shard_map/psum | solution.py:40
  66.4 5.9 copy-start.5
  66.4 6.0 copy-start.6
  82.8 198.8 %copy-start.3 = (bf16[1,64,1792]{2,1,0:T(8,128)(2,1)S(1)}, bf16[1,64,1792]{2,1,0:T(8,128)(2,1)}, u32[]{:S(2)}) copy-start(bf16[1,64,1792]{2,1,0:T(8,128)(2,1)} %param.10) | copy-start | bytes 688132
  82.8 198.8 %copy-start.4 = (bf16[1,64,1792]{2,1,0:T(8,128)(2,1)S(1)}, bf16[1,64,1792]{2,1,0:T(8,128)(2,1)}, u32[]{:S(2)}) copy-start(bf16[1,64,1792]{2,1,0:T(8,128)(2,1)} %param.9) | copy-start | bytes 688132
  82.8 628.6 %all-gather.9.cloned.1.call-start = ((), (), s32[]{:S(2)}) async-start(), calls=%async_computation.7 | async-start | bytes 3899392 | tf_op jit(solution)/shard_map/all_gather | solution.py:54
  283.7 523.7 %all-gather.7.cloned.1.call-start = ((), (), s32[]{:S(2)}) async-start(), calls=%async_computation.6 | async-start | bytes 3899392 | tf_op jit(solution)/shard_map/all_gather | solution.py:54
  284.2 559.5 %reduce-scatter.4.cloned.1.call-start = ((), (), s32[]{:S(2)}) async-start(), calls=%async_computation.4 | async-start | bytes 2359296 | tf_op jit(solution)/shard_map/reduce_scatter | solution.py:16
  629.1 252.3 %reduce-scatter.8.cloned.1.call-start = ((), (), s32[]{:S(2)}) async-start(), calls=%async_computation.8 | async-start | bytes 2359296 | tf_op jit(solution)/shard_map/reduce_scatter | solution.py:16
  717.5 126.2 %copy-start.1 = (bf16[1,128,512]{2,1,0:T(8,128)(2,1)S(1)}, bf16[1,128,512]{2,1,0:T(8,128)(2,1)}, u32[]{:S(2)}) copy-start(bf16[1,128,512]{2,1,0:T(8,128)(2,1)} %param.7) | copy-start | bytes 393220
  717.5 163.9 %copy-start.2 = (bf16[1,128,512]{2,1,0:T(8,128)(2,1)S(1)}, bf16[1,128,512]{2,1,0:T(8,128)(2,1)}, u32[]{:S(2)}) copy-start(bf16[1,128,512]{2,1,0:T(8,128)(2,1)} %param.8) | copy-start | bytes 393220
  882.6 5.1 collective-permute-start
Sparse Core Ops, SparseCore 0:
  9.9 28.7 all-gather.12
  40.5 25.7 all-gather.10
  70.4 211.2 reduce-scatter.5
  284.4 325.7 all-reduce.1
  613.0 98.4 all-gather.8
  714.3 93.0 all-gather.6
  810.1 33.5 reduce-scatter.3
  846.4 34.9 reduce-scatter.7
where the time goes:
time: 895 us
  waiting for transfers between devices  820 us (92%)
  matrix products  36.3 us (4%)
  other arithmetic  23.3 us (3%)
  between operations  14.2 us (2%)
    psum x1, waiting for transfers between devices, local(): total = lax.psum(both.astype(jnp.bfloat16), 'dp').astype(jnp.float32)  326 us
    reduce_scatter x1, waiting for transfers between devices, local(): lax.psum_scatter(transposed(all_grads, w_down).astype(jnp.bfloat16), 'dp'...  199 us
    all_gather x2, waiting for transfers between devices, local(): pieces = lax.all_gather((gate_grad, up_grad), 'dp', axis=0, tiled=True)  172 us
    reduce_scatter x2, waiting for transfers between devices, feature_total(): return lax.psum_scatter(term, 'tensor', scatter_dimension=0, tiled=True)  65.7 us
    all_gather x2, waiting for transfers between devices, across_rows(): return lax.all_gather(part, 'tensor', axis=0, tiled=True)  52.3 us
    dot_general x3, matrix products, transposed(): lax.dot_general(left, right, (((1,), (1,)), ((), ())), preferred_element_...  17.9 us
  transfers between devices with their start and end apart: 9, of which 9 were waited for; matrix products, arithmetic and copies ran while one was open for 7% of the time, Pallas kernels for 0%

commit v1 on v0

--- a/solution.py
+++ b/solution.py
@@ -2,6 +2,22 @@
 import jax.numpy as jnp
 from jax import lax
 from jax.sharding import PartitionSpec as P
+
+
+def collect(x, axis, dim):
+    ways, here, lap = (lax.axis_size(axis), lax.axis_index(axis), x.shape[dim])
+    shape = [n * ways if d == dim else n for d, n in enumerate(x.shape)]
+    full = lax.dynamic_update_slice_in_dim(jnp.zeros(shape, x.dtype), x, here * lap, axis=dim)
+    going_up = going_down = x
+    for far in range(1, ways // 2 + 1):
+        going_up = lax.ppermute(going_up, axis, [(d, (d + 1) % ways) for d in range(ways)])
+        full = lax.dynamic_update_slice_in_dim(full, going_up, (here - far) % ways * lap, axis=dim)
+        if 2 * far < ways:
+            going_down = lax.ppermute(going_down, axis, [(d, (d - 1) % ways) for d in range(ways)])
+            full = lax.dynamic_update_slice_in_dim(
+                full, going_down, (here + far) % ways * lap, axis=dim
+            )
+    return full
 
 
 def partner(shard, axis, apart):
@@ -9,7 +25,7 @@
 
 
 def across_rows(part):
-    return lax.all_gather(part, "tensor", axis=0, tiled=True)
+    return collect(part, "tensor", 0)
 
 
 def feature_total(term):

time: 895 us -> 860 us (0.961)
  waiting for transfers between devices: 820 us -> 765 us
  starting transfers between devices: 0.98 us -> 18.8 us
    all_gather x2 -> x0, waiting for transfers between devices: 52.3 us -> none  [across_rows(): return lax.all_gather(part, 'tensor', axis=0, tiled=True)]
    reduce_scatter x1, waiting for transfers between devices: 199 us -> 172 us  [local(): lax.psum_scatter(transposed(all_grads, w_down).astype(jnp.bfloat16), 'dp'...]
    ppermute x0 -> x14, waiting for transfers between devices: none -> 25.9 us  [the longest x8 25.9 us: collect(): lax.ppermute(going_up, axis, [(d, (d + 1) % ways) for d in range(ways)])]
    ppermute x0 -> x14, starting transfers between devices: none -> 17.8 us  [the longest x6 17.7 us: collect(): lax.ppermute(going_down, axis, [(d, (d - 1) % ways) for d in range(ways)])]
  transfers between devices with their start and end apart: 9 -> 21, of which waited for: 9 -> 15; matrix products, arithmetic and copies ran while one was open for 7% -> 6% of each run, Pallas kernels for 0% -> 0%
where the time goes in v1:
time: 860 us; the launch traced here: 859 us
  waiting for transfers between devices  765 us (89%)
  matrix products  34.8 us (4%)
  other arithmetic  23.3 us (3%)
  starting transfers between devices  18.8 us (2%)
  between operations  14.3 us (2%)
    psum x1, waiting for transfers between devices, local(): total = lax.psum(both.astype(jnp.bfloat16), 'dp').astype(jnp.float32)  326 us
    all_gather x2, waiting for transfers between devices, local(): pieces = lax.all_gather((gate_grad, up_grad), 'dp', axis=0, tiled=True)  172 us
    reduce_scatter x1, waiting for transfers between devices, local(): lax.psum_scatter(transposed(all_grads, w_down).astype(jnp.bfloat16), 'dp'...  172 us
    reduce_scatter x2, waiting for transfers between devices, feature_total(): return lax.psum_scatter(term, 'tensor', scatter_dimension=0, tiled=True)  65.5 us
    ppermute x8, waiting for transfers between devices, collect(): lax.ppermute(going_up, axis, [(d, (d + 1) % ways) for d in range(ways)])  25.9 us
    ppermute x6, starting transfers between devices, collect(): lax.ppermute(going_down, axis, [(d, (d - 1) % ways) for d in range(ways)])  17.7 us
  transfers between devices with their start and end apart: 21, of which 15 were waited for; matrix products, arithmetic and copies ran while one was open for 6% of the time, Pallas kernels for 0%

profile of v1, /device:TPU:8, one launch (start us, length us, event | category | flops | bytes accessed | tf_op | source)
XLA Modules:
  0.0 859.3 jit_solution(4341206345804964824)
XLA Ops:
  7.3 2.9 collective-permute-start.8
  11.2 1.9 collective-permute-done.7
  13.1 3.0 collective-permute-start.10
  16.1 2.6 collective-permute-done.9
  18.7 3.0 collective-permute-start.12
  21.7 2.6 collective-permute-done.11
  24.3 5.5 collective-permute-done.13
  29.9 4.0 convolution_convert_fusion
  34.8 3.0 collective-permute-start.1
  37.9 2.5 collective-permute-done
  40.5 3.0 collective-permute-start.3
  43.4 2.6 collective-permute-done.2
  46.1 3.0 collective-permute-start.5
  49.0 2.6 collective-permute-done.4
  51.7 5.5 collective-permute-done.6
  57.3 5.6 convolution_convert_fusion.1
  62.9 3.9 convolution_convert_fusion.2
  66.8 6.7 pad_maximum_fusion
  73.5 172.1 %reduce-scatter.6.cloned.1.call-done = bf16[64,1792]{1,0:T(8,128)(2,1)} async-done(((bf16[1024,1792]{1,0:T(8,128)(2,1)}), bf16[64,1792]{1,0:T(8,128)(2,1)}) %reduce-scatter.6.cloned.1.call-update) | async-done | bytes 229392 | tf_op jit(solution)/shard_map/reduce_scatter | solution.py:62
  245.6 2.0 fusion.16
  248.2 326.3 %all-reduce.2.cloned.1.call-done = bf16[1024,3584]{1,0:T(8,128)(2,1)} async-done(((bf16[1024,3584]{1,0:T(8,128)(2,1)}), bf16[1024,3584]{1,0:T(8,128)(2,1)}) %all-reduce.2.cloned.1.call-update) | async-done | bytes 7340048 | tf_op jit(solution)/shard_map/psum | solution.py:56
  574.5 10.3 %convert_element_type.44 = f32[1024,3584]{1,0:T(8,128)} convert(bf16[1024,3584]{1,0:T(8,128)(2,1)} %all-reduce.2.cloned.1.call-done) | non-fusion elementwise | flops 3670016 | bytes 22020096 | tf_op jit(solution)/shard_map/convert_element_type | solution.py:56
  584.8 8.6 fusion.1
  593.6 82.3 %all-gather.5.cloned.1.call-done = bf16[1024,1792]{1,0:T(8,128)(2,1)} async-done(((bf16[64,1792]{1,0:T(8,128)(2,1)}), bf16[1024,1792]{1,0:T(8,128)(2,1)}) %all-gather.5.cloned.1.call-update) | async-done | bytes 3670032 | tf_op jit(solution)/shard_map/all_gather | solution.py:70
  676.0 6.0 fusion.5
  682.0 89.9 %all-gather.3.cloned.1.call-done = bf16[1024,1792]{1,0:T(8,128)(2,1)} async-done(((bf16[64,1792]{1,0:T(8,128)(2,1)}), bf16[1024,1792]{1,0:T(8,128)(2,1)}) %all-gather.3.cloned.1.call-update) | async-done | bytes 3670032 | tf_op jit(solution)/shard_map/all_gather | solution.py:70
  771.9 6.7 fusion.11
  778.6 29.5 %reduce-scatter.4.cloned.1.call-done = f32[128,512]{1,0:T(8,128)} async-done(((f32[1024,512]{1,0:T(8,128)}), f32[128,512]{1,0:T(8,128)}) %reduce-scatter.4.cloned.1.call-update) | async-done | bytes 262160 | tf_op jit(solution)/shard_map/reduce_scatter | solution.py:32
  808.0 1.6 fusion.24
  809.6 36.0 %reduce-scatter.8.cloned.1.call-done = f32[128,512]{1,0:T(8,128)} async-done(((f32[1024,512]{1,0:T(8,128)}), f32[128,512]{1,0:T(8,128)}) %reduce-scatter.8.cloned.1.call-update) | async-done | bytes 262160 | tf_op jit(solution)/shard_map/reduce_scatter | solution.py:32
  847.4 1.6 fusion.25
  849.0 2.8 collective-permute-done.14
  (59 shorter events, 5.5 us)
Async XLA Ops:
  7.2 22.7 %copy-start = (bf16[1,1792,512]{2,1,0:T(8,128)(2,1)S(1)}, bf16[1,1792,512]{2,1,0:T(8,128)(2,1)}, u32[]{:S(2)}) copy-start(bf16[1,1792,512]{2,1,0:T(8,128)(2,1)} %param.13) | copy-start | bytes 5505028
  7.2 238.4 %reduce-scatter.6.cloned.1.call-start = ((), (), s32[]{:S(2)}) async-start(), calls=%async_computation.5 | async-start | bytes 3899392 | tf_op jit(solution)/shard_map/reduce_scatter | solution.py:62
  7.2 5.8 collective-permute-start.7
  7.3 5.8 collective-permute-start.8
  13.1 5.6 collective-permute-start.9
  13.1 5.6 collective-permute-start.10
  18.7 5.6 collective-permute-start.11
  18.7 5.6 collective-permute-start.12
  24.3 5.6 collective-permute-start.13
  33.9 0.9 copy-start.1
  33.9 540.6 %all-reduce.2.cloned.1.call-start = ((), (), s32[]{:S(2)}) async-start(), calls=%async_computation.3 | async-start | bytes 14680064 | tf_op jit(solution)/shard_map/psum | solution.py:56
  34.8 5.6 collective-permute-start
  34.8 5.6 collective-permute-start.1
  40.4 5.6 collective-permute-start.2
  40.5 5.6 collective-permute-start.3
  46.0 5.6 collective-permute-start.4
  46.1 5.6 collective-permute-start.5
  51.6 5.6 collective-permute-start.6
  57.3 5.6 copy-start.5
  73.4 172.2 %copy-start.3 = (bf16[1,64,1792]{2,1,0:T(8,128)(2,1)S(1)}, bf16[1,64,1792]{2,1,0:T(8,128)(2,1)}, u32[]{:S(2)}) copy-start(bf16[1,64,1792]{2,1,0:T(8,128)(2,1)} %param.10) | copy-start | bytes 688132
  73.4 172.2 %copy-start.4 = (bf16[1,64,1792]{2,1,0:T(8,128)(2,1)S(1)}, bf16[1,64,1792]{2,1,0:T(8,128)(2,1)}, u32[]{:S(2)}) copy-start(bf16[1,64,1792]{2,1,0:T(8,128)(2,1)} %param.9) | copy-start | bytes 688132
  73.4 602.5 %all-gather.5.cloned.1.call-start = ((), (), s32[]{:S(2)}) async-start(), calls=%async_computation.7 | async-start | bytes 3899392 | tf_op jit(solution)/shard_map/all_gather | solution.py:70
  247.6 524.2 %all-gather.3.cloned.1.call-start = ((), (), s32[]{:S(2)}) async-start(), calls=%async_computation.6 | async-start | bytes 3899392 | tf_op jit(solution)/shard_map/all_gather | solution.py:70
  248.2 559.8 %reduce-scatter.4.cloned.1.call-start = ((), (), s32[]{:S(2)}) async-start(), calls=%async_computation.4 | async-start | bytes 2359296 | tf_op jit(solution)/shard_map/reduce_scatter | solution.py:32
  593.4 252.3 %reduce-scatter.8.cloned.1.call-start = ((), (), s32[]{:S(2)}) async-start(), calls=%async_computation.8 | async-start | bytes 2359296 | tf_op jit(solution)/shard_map/reduce_scatter | solution.py:32
  682.0 163.7 %copy-start.2 = (bf16[1,128,512]{2,1,0:T(8,128)(2,1)S(1)}, bf16[1,128,512]{2,1,0:T(8,128)(2,1)}, u32[]{:S(2)}) copy-start(bf16[1,128,512]{2,1,0:T(8,128)(2,1)} %param.8) | copy-start | bytes 393220
  846.8 5.1 collective-permute-start.14
Sparse Core Ops, SparseCore 0:
  34.1 211.4 reduce-scatter.5
  248.5 325.9 all-reduce.1
  577.4 98.4 all-gather.4
  678.7 93.0 all-gather.2
  774.4 33.5 reduce-scatter.3
  810.6 35.0 reduce-scatter.7
